TPU v7x, 1024 devices: a whole 4x8x16 slice. The times are simulated.
1024 devices in a mesh: gx: 32 (over y_lo, z), gy: 32 (over x, y_hi, core).
Axes of the slice: x: 4, y: 8 (y_hi: 4, y_lo: 2; y = y_hi * 2 + y_lo), z: 16, core: 2. Of those that a mesh axis runs over, the one named last changes fastest.
Arguments:
- hamiltonian: float32 [32, 32, 5, 128, 128], P('gx', 'gy'), may hold values from -0.25 to 0.25
- inverse_margin: float32 [32, 32, 5, 128, 128], P('gx', 'gy'), may hold values from -0.25 to 0.25
- density: float32 [2, 32, 32, 5, 128, 128], P(None, 'gx', 'gy'), may hold values from -6 to 6
- cutoff: int32 [32, 32, 5], P('gx', 'gy'), may hold values 0 or 1
- derivative: float32 [3, 32, 32, 5, 128, 128], P(None, 'gx', 'gy'), may hold values from -0.046875 to 0.046875
- atom_of: int32 [32, 32, 128], P('gx', 'gy'), may hold values from 0 to 63, as said below
Outputs:
- new_density: float32 [2, 32, 32, 5, 128, 128], P(None, 'gx', 'gy')
- forces: float32 [32, 32, 3, 64], P('gx', 'gy')
Inputs may be any that keep to these rules, and one draw needn't show every extreme that they name: `atom_of`: within each group the map never falls and each of the 64 atoms owns at least one of the 128 orbitals.
All inputs are finite; a program needn't handle non-finite values. No bound on the sum of `cutoff` on one device may be relied on, other than what follows from the above.
Results may differ from a plain program's by a relative error of at most 0.0001.
Values sent between devices are 32-bit elements; how exact they have to be, the bound alone decides.
A program may use at most 64 MiB of HBM per device.

v0:
```python
import jax
import jax.numpy as jnp
from jax import lax
from jax.sharding import PartitionSpec as P

ATOMS = 64


opposite = (0, 2, 1, 4, 3)
time_step = 0.25
highest = lax.Precision.HIGHEST
positions = ((2, 1), (0, 1), (1, 2), (1, 0))


def padded_2(cells, sides, width):
    for axis, dim in sides:
        count = lax.axis_size(axis)
        head = lax.slice_in_dim(cells, 0, width, axis=dim)
        tail = lax.slice_in_dim(cells, cells.shape[dim] - width, cells.shape[dim], axis=dim)
        cells = jnp.concatenate(
            [
                lax.ppermute(tail, axis, [(i, (i + 1) % count) for i in range(count)]),
                cells,
                lax.ppermute(head, axis, [((i + 1) % count, i) for i in range(count)]),
            ],
            axis=dim,
        )
    return cells


def neighbours(padded):
    zero_blocks = jnp.stack(
        [padded[..., first_at, second_at, 0, :, :] for first_at, second_at in positions], axis=-3
    )
    back_blocks = jnp.stack(
        [
            padded[..., spot[0], spot[1], opposite[place + 1], :, :]
            for place, spot in enumerate(positions)
        ],
        axis=-3,
    )
    return (zero_blocks, back_blocks)


def matmul(left, right):
    return jnp.matmul(left, right, precision=highest)


def product(left, right, zero_blocks, back_blocks, keep):
    joined = jnp.concatenate([right[..., :1, :, :], back_blocks], axis=-3)
    diagonal = jnp.sum(matmul(left, joined), axis=-3)
    others = matmul(left[..., :1, :, :], right[..., 1:, :, :]) + matmul(
        left[..., 1:, :, :], zero_blocks
    )
    result = jnp.concatenate([diagonal[..., None, :, :], others], axis=-3)
    return result * keep[:, None, None]


def density_neighbours(current):
    padded = padded_2(current[:, None, None], (("gx", 1), ("gy", 2)), 1)
    return neighbours(padded)


def local(hamiltonian, inverse_margin, density, cutoff, derivative, atom_of):
    keep = jnp.concatenate([jnp.ones((1,), jnp.float32), cutoff[0, 0, 1:].astype(jnp.float32)])
    weight = keep[:, None, None]
    ham = hamiltonian[0, 0] * weight
    inverse = inverse_margin[0, 0] * weight
    stacked = jnp.stack([ham, inverse], axis=0)[:, None, None]
    padded = padded_2(stacked, (("gx", 1), ("gy", 2)), 1)
    near_zero, near_back = neighbours(padded)
    propagator = product(inverse, ham, near_zero[0], near_back[0], keep)
    current = density[:, 0, 0] * weight[None]
    rho_zero, rho_back = density_neighbours(current)
    left_term = product(propagator, current, rho_zero, rho_back, keep)
    mixed = product(current, ham, near_zero[0], near_back[0], keep)
    right_term = product(mixed, inverse, near_zero[1], near_back[1], keep)
    commutators = left_term - right_term
    current = jnp.stack(
        [current[0] + time_step * commutators[1], current[1] - time_step * commutators[0]], axis=0
    )
    slopes = derivative[:, 0, 0] * weight[None]
    weighted = current[0][None] * slopes
    row_part = jnp.sum(weighted, axis=(1, 3))
    column_part = jnp.sum(weighted, axis=2)
    received = padded_2(column_part[None, None], (("gx", 0), ("gy", 1)), 1)
    orbital = row_part + column_part[:, 0]
    orbital = (
        orbital
        + received[0, 1, :, 1]
        + received[2, 1, :, 2]
        + received[1, 0, :, 3]
        + received[1, 2, :, 4]
    )
    members = (atom_of[0, 0][None, :] == jnp.arange(ATOMS, dtype=jnp.int32)[:, None]).astype(
        jnp.float32
    )
    forces = -jnp.einsum("cw,aw->ca", orbital, members, precision=highest)
    return (current[:, None, None], forces[None, None])


def solution(mesh):
    placed = (
        P("gx", "gy", None, None, None),
        P("gx", "gy", None, None, None),
        P(None, "gx", "gy", None, None, None),
        P("gx", "gy", None),
        P(None, "gx", "gy", None, None, None),
        P("gx", "gy", None),
    )
    return jax.shard_map(
        local,
        mesh=mesh,
        in_specs=placed,
        out_specs=(P(None, "gx", "gy", None, None, None), P("gx", "gy", None, None)),
        check_vma=False,
    )
```

profile of v0, /device:TPU:8, one launch (start us, length us, event | category | flops | bytes accessed | tf_op | source)
XLA Modules:
  0.0 172.4 jit_solution(15817857617181103044)
XLA Ops:
  0.6 0.0 copy-start
  0.6 0.8 convert_bitcast_fusion
  1.4 0.1 pad_maximum_fusion.9
  1.5 1.2 bitcast_multiply_fusion.3
  2.7 0.0 copy-start.1
  2.7 0.0 copy-start.2
  2.8 18.2 %collective-permute-start = (f32[2,1,1,5,128,128]{5,4,0,3,2,1:T(8,128)S(1)}, f32[2,1,1,5,128,128]{5,4,0,3,2,1:T(8,128)S(1)}, u32[]{:S(2)}, u32[]{:S(2)}) collective-permute-start(f32[2,1,1,5,128,128]{5,4,0,3,2,1:T(8,128)S(1)} %maximum_bitcast_fusion), channel_id=1, source_target_pairs={{32,0},{64,32},{96,64},{128,96},{160,128},{192,160},{224,192},{256... | collective-permute-start | bytes 1966088 | tf_op jit(solution)/shard_map/ppermute | solution.py:24
  21.0 1.9 %collective-permute-start.1 = (f32[2,1,1,5,128,128]{5,4,0,3,2,1:T(8,128)S(1)}, f32[2,1,1,5,128,128]{5,4,0,3,2,1:T(8,128)S(1)}, u32[]{:S(2)}, u32[]{:S(2)}) collective-permute-start(f32[2,1,1,5,128,128]{5,4,0,3,2,1:T(8,128)S(1)} %maximum_bitcast_fusion), channel_id=1, source_target_pairs={{0,32},{32,64},{64,96},{96,128},{128,160},{160,192},{192,224},{224... | collective-permute-start | bytes 1966088 | tf_op jit(solution)/shard_map/ppermute | solution.py:22
  23.0 0.0 copy-done
  23.0 0.1 copy_multiply_fusion
  23.1 6.0 %collective-permute-start.4 = (f32[2,1,1,5,128,128]{5,4,0,3,2,1:T(8,128)S(1)}, f32[2,1,1,5,128,128]{5,4,0,3,2,1:T(8,128)S(1)}, u32[]{:S(2)}, u32[]{:S(2)}) collective-permute-start(f32[2,1,1,5,128,128]{5,4,0,3,2,1:T(8,128)S(1)} %copy_multiply_fusion), channel_id=1, source_target_pairs={{32,0},{64,32},{96,64},{128,96},{160,128},{192,160},{224,192},{256... | collective-permute-start | bytes 1966088 | tf_op jit(solution)/shard_map/ppermute | solution.py:24
  29.1 1.9 %collective-permute-start.5 = (f32[2,1,1,5,128,128]{5,4,0,3,2,1:T(8,128)S(1)}, f32[2,1,1,5,128,128]{5,4,0,3,2,1:T(8,128)S(1)}, u32[]{:S(2)}, u32[]{:S(2)}) collective-permute-start(f32[2,1,1,5,128,128]{5,4,0,3,2,1:T(8,128)S(1)} %copy_multiply_fusion), channel_id=1, source_target_pairs={{0,32},{32,64},{64,96},{96,128},{128,160},{160,192},{192,224},{224... | collective-permute-start | bytes 1966088 | tf_op jit(solution)/shard_map/ppermute | solution.py:22
  31.1 0.1 bitcast_multiply_fusion.1
  31.2 0.0 copy-done.1
  31.2 0.0 copy-done.2
  31.2 0.1 bitcast_multiply_fusion.5
  31.4 4.8 %collective-permute-done = f32[2,1,1,5,128,128]{5,4,0,3,2,1:T(8,128)S(1)} collective-permute-done((f32[2,1,1,5,128,128]{5,4,0,3,2,1:T(8,128)S(1)}, f32[2,1,1,5,128,128]{5,4,0,3,2,1:T(8,128)S(1)}, u32[]{:S(2)}, u32[]{:S(2)}) %collective-permute-start) | collective-permute-done | bytes 655392 | tf_op jit(solution)/shard_map/ppermute | solution.py:24
  36.2 6.5 %collective-permute-done.1 = f32[2,1,1,5,128,128]{5,4,0,3,2,1:T(8,128)S(1)} collective-permute-done((f32[2,1,1,5,128,128]{5,4,0,3,2,1:T(8,128)S(1)}, f32[2,1,1,5,128,128]{5,4,0,3,2,1:T(8,128)S(1)}, u32[]{:S(2)}, u32[]{:S(2)}) %collective-permute-start.1) | collective-permute-done | bytes 655392 | tf_op jit(solution)/shard_map/ppermute | solution.py:22
  42.7 0.2 pad_maximum_fusion
  42.9 1.9 %collective-permute-start.3 = (f32[2,3,1,5,128,128]{5,4,0,3,2,1:T(8,128)S(1)}, f32[2,3,1,5,128,128]{5,4,0,3,2,1:T(8,128)S(1)}, u32[]{:S(2)}, u32[]{:S(2)}) collective-permute-start(f32[2,3,1,5,128,128]{5,4,0,3,2,1:T(8,128)S(1)} %pad_maximum_fusion), channel_id=1, source_target_pairs={{0,1},{1,2},{2,3},{3,4},{4,5},{5,6},{6,7},{7,8},{8,9},{9,10},{10,1... | collective-permute-start | bytes 5898248 | tf_op jit(solution)/shard_map/ppermute | solution.py:22
  44.8 0.4 convolution_bitcast_fusion.6
  45.2 7.9 %collective-permute-start.2 = (f32[2,3,1,5,128,128]{5,4,0,3,2,1:T(8,128)S(1)}, f32[2,3,1,5,128,128]{5,4,0,3,2,1:T(8,128)S(1)}, u32[]{:S(2)}, u32[]{:S(2)}) collective-permute-start(f32[2,3,1,5,128,128]{5,4,0,3,2,1:T(8,128)S(1)} %pad_maximum_fusion), channel_id=1, source_target_pairs={{1,0},{2,1},{3,2},{4,3},{5,4},{6,5},{7,6},{8,7},{9,8},{10,9},{11,1... | collective-permute-start | bytes 5898248 | tf_op jit(solution)/shard_map/ppermute | solution.py:24
  53.1 0.0 collective-permute-done.4
  53.1 6.7 %collective-permute-done.5 = f32[2,1,1,5,128,128]{5,4,0,3,2,1:T(8,128)S(1)} collective-permute-done((f32[2,1,1,5,128,128]{5,4,0,3,2,1:T(8,128)S(1)}, f32[2,1,1,5,128,128]{5,4,0,3,2,1:T(8,128)S(1)}, u32[]{:S(2)}, u32[]{:S(2)}) %collective-permute-start.5) | collective-permute-done | bytes 655392 | tf_op jit(solution)/shard_map/ppermute | solution.py:22
  59.8 0.2 pad_maximum_fusion.1
  60.0 5.4 %collective-permute-start.6 = (f32[2,3,1,5,128,128]{5,4,0,3,2,1:T(8,128)S(1)}, f32[2,3,1,5,128,128]{5,4,0,3,2,1:T(8,128)S(1)}, u32[]{:S(2)}, u32[]{:S(2)}) collective-permute-start(f32[2,3,1,5,128,128]{5,4,0,3,2,1:T(8,128)S(1)} %pad_maximum_fusion.1), channel_id=1, source_target_pairs={{1,0},{2,1},{3,2},{4,3},{5,4},{6,5},{7,6},{8,7},{9,8},{10,9},{11,1... | collective-permute-start | bytes 5898248 | tf_op jit(solution)/shard_map/ppermute | solution.py:24
  65.5 1.9 %collective-permute-start.7 = (f32[2,3,1,5,128,128]{5,4,0,3,2,1:T(8,128)S(1)}, f32[2,3,1,5,128,128]{5,4,0,3,2,1:T(8,128)S(1)}, u32[]{:S(2)}, u32[]{:S(2)}) collective-permute-start(f32[2,3,1,5,128,128]{5,4,0,3,2,1:T(8,128)S(1)} %pad_maximum_fusion.1), channel_id=1, source_target_pairs={{0,1},{1,2},{2,3},{3,4},{4,5},{5,6},{6,7},{7,8},{8,9},{9,10},{10,1... | collective-permute-start | bytes 5898248 | tf_op jit(solution)/shard_map/ppermute | solution.py:22
  67.5 11.1 %collective-permute-done.3 = f32[2,3,1,5,128,128]{5,4,0,3,2,1:T(8,128)S(1)} collective-permute-done((f32[2,3,1,5,128,128]{5,4,0,3,2,1:T(8,128)S(1)}, f32[2,3,1,5,128,128]{5,4,0,3,2,1:T(8,128)S(1)}, u32[]{:S(2)}, u32[]{:S(2)}) %collective-permute-start.3) | collective-permute-done | bytes 1966112 | tf_op jit(solution)/shard_map/ppermute | solution.py:22
  78.7 38.9 %collective-permute-done.2 = f32[2,3,1,5,128,128]{5,4,0,3,2,1:T(8,128)S(1)} collective-permute-done((f32[2,3,1,5,128,128]{5,4,0,3,2,1:T(8,128)S(1)}, f32[2,3,1,5,128,128]{5,4,0,3,2,1:T(8,128)S(1)}, u32[]{:S(2)}, u32[]{:S(2)}) %collective-permute-start.2) | collective-permute-done | bytes 1966112 | tf_op jit(solution)/shard_map/ppermute | solution.py:24
  117.6 0.1 pad_maximum_fusion.3
  117.7 0.5 convolution_bitcast_fusion.10
  118.2 0.4 convolution_add_fusion
  118.6 20.0 %collective-permute-done.6 = f32[2,3,1,5,128,128]{5,4,0,3,2,1:T(8,128)S(1)} collective-permute-done((f32[2,3,1,5,128,128]{5,4,0,3,2,1:T(8,128)S(1)}, f32[2,3,1,5,128,128]{5,4,0,3,2,1:T(8,128)S(1)}, u32[]{:S(2)}, u32[]{:S(2)}) %collective-permute-start.6) | collective-permute-done | bytes 1966112 | tf_op jit(solution)/shard_map/ppermute | solution.py:24
  138.7 0.1 maximum_multiply_fusion.3
  138.7 0.7 convolution_bitcast_fusion.8
  139.4 0.6 convolution_bitcast_fusion.5
  140.1 0.6 fusion.1
  140.6 0.1 maximum_multiply_fusion.1
  140.8 0.6 convolution_bitcast_fusion.4
  141.4 0.6 fusion.2
  142.0 0.0 collective-permute-done.7
  142.0 0.5 convolution_bitcast_fusion.9
  142.5 0.6 convolution_bitcast_fusion.2
  143.1 0.6 fusion
  143.7 0.7 convolution_bitcast_fusion.7
  144.4 0.0 copy-start.3
  144.4 0.1 fusion.7
  144.6 0.0 copy-start.4
  144.6 0.1 fusion.11
  144.7 0.9 copy-done.3
  145.6 0.3 fusion.6
  145.9 1.9 %collective-permute-start.8 = (f32[1,1,3,5,128]{4,2,3,1,0:T(4,128)S(1)}, f32[1,1,3,5,128]{4,2,3,1,0:T(4,128)S(1)}, u32[]{:S(2)}, u32[]{:S(2)}) collective-permute-start(f32[1,1,3,5,128]{4,2,3,1,0:T(4,128)S(1)} %copy.35), channel_id=1, source_target_pairs={{0,32},{32,64},{64,96},{96,128},{128,160},{160,192},{192,224},{224... | collective-permute-start | bytes 23048 | tf_op jit(solution)/shard_map/ppermute | solution.py:22
  147.8 6.0 %collective-permute-start.9 = (f32[1,1,3,5,128]{4,2,3,1,0:T(4,128)S(1)}, f32[1,1,3,5,128]{4,2,3,1,0:T(4,128)S(1)}, u32[]{:S(2)}, u32[]{:S(2)}) collective-permute-start(f32[1,1,3,5,128]{4,2,3,1,0:T(4,128)S(1)} %copy.35), channel_id=1, source_target_pairs={{32,0},{64,32},{96,64},{128,96},{160,128},{192,160},{224,192},{256... | collective-permute-start | bytes 23048 | tf_op jit(solution)/shard_map/ppermute | solution.py:24
  153.9 0.0 collective-permute-done.8
  153.9 1.3 collective-permute-done.9
  155.3 6.9 %collective-permute-start.11 = (f32[3,1,3,5,128]{4,3,2,1,0:T(8,128)S(1)}, f32[3,1,3,5,128]{4,3,2,1,0:T(8,128)S(1)}, u32[]{:S(2)}, u32[]{:S(2)}) collective-permute-start(f32[3,1,3,5,128]{4,3,2,1,0:T(8,128)S(1)} %pad_maximum_fusion.8), channel_id=1, source_target_pairs={{1,0},{2,1},{3,2},{4,3},{5,4},{6,5},{7,6},{8,7},{9,8},{10,9},{11,1... | collective-permute-start | bytes 69128 | tf_op jit(solution)/shard_map/ppermute | solution.py:24
  162.2 1.9 %collective-permute-start.10 = (f32[3,1,3,5,128]{4,2,3,1,0:T(4,128)S(1)}, f32[3,1,3,5,128]{4,2,3,1,0:T(4,128)S(1)}, u32[]{:S(2)}, u32[]{:S(2)}) collective-permute-start(f32[3,1,3,5,128]{4,2,3,1,0:T(4,128)S(1)} %copy.39), channel_id=1, source_target_pairs={{0,1},{1,2},{2,3},{3,4},{4,5},{5,6},{6,7},{7,8},{8,9},{9,10},{10,1... | collective-permute-start | bytes 69128 | tf_op jit(solution)/shard_map/ppermute | solution.py:22
  164.1 0.9 maximum_bitcast_fusion.1
  165.0 0.0 collective-permute-done.11
  165.0 6.6 %collective-permute-done.10 = f32[3,1,3,5,128]{4,2,3,1,0:T(4,128)S(1)} collective-permute-done((f32[3,1,3,5,128]{4,2,3,1,0:T(4,128)S(1)}, f32[3,1,3,5,128]{4,2,3,1,0:T(4,128)S(1)}, u32[]{:S(2)}, u32[]{:S(2)}) %collective-permute-start.10) | collective-permute-done | bytes 23072 | tf_op jit(solution)/shard_map/ppermute | solution.py:22
  171.6 0.0 copy-done.4
  171.6 0.1 fusion.3
  171.7 0.6 copy.41
  (25 shorter events, 0.3 us)
Async XLA Ops:
  0.6 22.3 %copy-start = (f32[2,1,1,5,128,128]{5,4,3,2,1,0:T(8,128)S(1)}, f32[2,1,1,5,128,128]{5,4,3,2,1,0:T(8,128)}, u32[]{:S(2)}) copy-start(f32[2,1,1,5,128,128]{5,4,3,2,1,0:T(8,128)} %param.8) | copy-start | bytes 1966084
  2.7 28.5 %copy-start.1 = (f32[1,1,5,128,128]{4,3,2,1,0:T(8,128)S(1)}, f32[1,1,5,128,128]{4,3,2,1,0:T(8,128)}, u32[]{:S(2)}) copy-start(f32[1,1,5,128,128]{4,3,2,1,0:T(8,128)} %param.7) | copy-start | bytes 983044
  2.7 28.5 %copy-start.2 = (f32[1,1,5,128,128]{4,3,2,1,0:T(8,128)S(1)}, f32[1,1,5,128,128]{4,3,2,1,0:T(8,128)}, u32[]{:S(2)}) copy-start(f32[1,1,5,128,128]{4,3,2,1,0:T(8,128)} %param.6) | copy-start | bytes 983044
  2.8 33.4 %collective-permute-start = (f32[2,1,1,5,128,128]{5,4,0,3,2,1:T(8,128)S(1)}, f32[2,1,1,5,128,128]{5,4,0,3,2,1:T(8,128)S(1)}, u32[]{:S(2)}, u32[]{:S(2)}) collective-permute-start(f32[2,1,1,5,128,128]{5,4,0,3,2,1:T(8,128)S(1)} %maximum_bitcast_fusion), channel_id=1, source_target_pairs={{32,0},{64,32},{96,64},{128,96},{160,128},{192,160},{224,192},{256... | collective-permute-start | bytes 1966088 | tf_op jit(solution)/shard_map/ppermute | solution.py:24
  21.0 21.7 %collective-permute-start.1 = (f32[2,1,1,5,128,128]{5,4,0,3,2,1:T(8,128)S(1)}, f32[2,1,1,5,128,128]{5,4,0,3,2,1:T(8,128)S(1)}, u32[]{:S(2)}, u32[]{:S(2)}) collective-permute-start(f32[2,1,1,5,128,128]{5,4,0,3,2,1:T(8,128)S(1)} %maximum_bitcast_fusion), channel_id=1, source_target_pairs={{0,32},{32,64},{64,96},{96,128},{128,160},{160,192},{192,224},{224... | collective-permute-start | bytes 1966088 | tf_op jit(solution)/shard_map/ppermute | solution.py:22
  23.1 30.0 %collective-permute-start.4 = (f32[2,1,1,5,128,128]{5,4,0,3,2,1:T(8,128)S(1)}, f32[2,1,1,5,128,128]{5,4,0,3,2,1:T(8,128)S(1)}, u32[]{:S(2)}, u32[]{:S(2)}) collective-permute-start(f32[2,1,1,5,128,128]{5,4,0,3,2,1:T(8,128)S(1)} %copy_multiply_fusion), channel_id=1, source_target_pairs={{32,0},{64,32},{96,64},{128,96},{160,128},{192,160},{224,192},{256... | collective-permute-start | bytes 1966088 | tf_op jit(solution)/shard_map/ppermute | solution.py:24
  29.1 30.7 %collective-permute-start.5 = (f32[2,1,1,5,128,128]{5,4,0,3,2,1:T(8,128)S(1)}, f32[2,1,1,5,128,128]{5,4,0,3,2,1:T(8,128)S(1)}, u32[]{:S(2)}, u32[]{:S(2)}) collective-permute-start(f32[2,1,1,5,128,128]{5,4,0,3,2,1:T(8,128)S(1)} %copy_multiply_fusion), channel_id=1, source_target_pairs={{0,32},{32,64},{64,96},{96,128},{128,160},{160,192},{192,224},{224... | collective-permute-start | bytes 1966088 | tf_op jit(solution)/shard_map/ppermute | solution.py:22
  42.9 35.7 %collective-permute-start.3 = (f32[2,3,1,5,128,128]{5,4,0,3,2,1:T(8,128)S(1)}, f32[2,3,1,5,128,128]{5,4,0,3,2,1:T(8,128)S(1)}, u32[]{:S(2)}, u32[]{:S(2)}) collective-permute-start(f32[2,3,1,5,128,128]{5,4,0,3,2,1:T(8,128)S(1)} %pad_maximum_fusion), channel_id=1, source_target_pairs={{0,1},{1,2},{2,3},{3,4},{4,5},{5,6},{6,7},{7,8},{8,9},{9,10},{10,1... | collective-permute-start | bytes 5898248 | tf_op jit(solution)/shard_map/ppermute | solution.py:22
  45.2 72.4 %collective-permute-start.2 = (f32[2,3,1,5,128,128]{5,4,0,3,2,1:T(8,128)S(1)}, f32[2,3,1,5,128,128]{5,4,0,3,2,1:T(8,128)S(1)}, u32[]{:S(2)}, u32[]{:S(2)}) collective-permute-start(f32[2,3,1,5,128,128]{5,4,0,3,2,1:T(8,128)S(1)} %pad_maximum_fusion), channel_id=1, source_target_pairs={{1,0},{2,1},{3,2},{4,3},{5,4},{6,5},{7,6},{8,7},{9,8},{10,9},{11,1... | collective-permute-start | bytes 5898248 | tf_op jit(solution)/shard_map/ppermute | solution.py:24
  60.0 78.6 %collective-permute-start.6 = (f32[2,3,1,5,128,128]{5,4,0,3,2,1:T(8,128)S(1)}, f32[2,3,1,5,128,128]{5,4,0,3,2,1:T(8,128)S(1)}, u32[]{:S(2)}, u32[]{:S(2)}) collective-permute-start(f32[2,3,1,5,128,128]{5,4,0,3,2,1:T(8,128)S(1)} %pad_maximum_fusion.1), channel_id=1, source_target_pairs={{1,0},{2,1},{3,2},{4,3},{5,4},{6,5},{7,6},{8,7},{9,8},{10,9},{11,1... | collective-permute-start | bytes 5898248 | tf_op jit(solution)/shard_map/ppermute | solution.py:24
  65.5 76.5 %collective-permute-start.7 = (f32[2,3,1,5,128,128]{5,4,0,3,2,1:T(8,128)S(1)}, f32[2,3,1,5,128,128]{5,4,0,3,2,1:T(8,128)S(1)}, u32[]{:S(2)}, u32[]{:S(2)}) collective-permute-start(f32[2,3,1,5,128,128]{5,4,0,3,2,1:T(8,128)S(1)} %pad_maximum_fusion.1), channel_id=1, source_target_pairs={{0,1},{1,2},{2,3},{3,4},{4,5},{5,6},{6,7},{7,8},{8,9},{9,10},{10,1... | collective-permute-start | bytes 5898248 | tf_op jit(solution)/shard_map/ppermute | solution.py:22
  144.4 1.2 copy-start.3
  144.6 27.0 %copy-start.4 = (s32[1,1,128]{2,1,0:T(1,128)S(1)}, s32[1,1,128]{2,1,0:T(1,128)}, u32[]{:S(2)}) copy-start(s32[1,1,128]{2,1,0:T(1,128)} %param.11) | copy-start | bytes 1540
  145.9 8.0 %collective-permute-start.8 = (f32[1,1,3,5,128]{4,2,3,1,0:T(4,128)S(1)}, f32[1,1,3,5,128]{4,2,3,1,0:T(4,128)S(1)}, u32[]{:S(2)}, u32[]{:S(2)}) collective-permute-start(f32[1,1,3,5,128]{4,2,3,1,0:T(4,128)S(1)} %copy.35), channel_id=1, source_target_pairs={{0,32},{32,64},{64,96},{96,128},{128,160},{160,192},{192,224},{224... | collective-permute-start | bytes 23048 | tf_op jit(solution)/shard_map/ppermute | solution.py:22
  147.8 7.4 %collective-permute-start.9 = (f32[1,1,3,5,128]{4,2,3,1,0:T(4,128)S(1)}, f32[1,1,3,5,128]{4,2,3,1,0:T(4,128)S(1)}, u32[]{:S(2)}, u32[]{:S(2)}) collective-permute-start(f32[1,1,3,5,128]{4,2,3,1,0:T(4,128)S(1)} %copy.35), channel_id=1, source_target_pairs={{32,0},{64,32},{96,64},{128,96},{160,128},{192,160},{224,192},{256... | collective-permute-start | bytes 23048 | tf_op jit(solution)/shard_map/ppermute | solution.py:24
  155.3 9.7 %collective-permute-start.11 = (f32[3,1,3,5,128]{4,3,2,1,0:T(8,128)S(1)}, f32[3,1,3,5,128]{4,3,2,1,0:T(8,128)S(1)}, u32[]{:S(2)}, u32[]{:S(2)}) collective-permute-start(f32[3,1,3,5,128]{4,3,2,1,0:T(8,128)S(1)} %pad_maximum_fusion.8), channel_id=1, source_target_pairs={{1,0},{2,1},{3,2},{4,3},{5,4},{6,5},{7,6},{8,7},{9,8},{10,9},{11,1... | collective-permute-start | bytes 69128 | tf_op jit(solution)/shard_map/ppermute | solution.py:24
  162.2 9.4 %collective-permute-start.10 = (f32[3,1,3,5,128]{4,2,3,1,0:T(4,128)S(1)}, f32[3,1,3,5,128]{4,2,3,1,0:T(4,128)S(1)}, u32[]{:S(2)}, u32[]{:S(2)}) collective-permute-start(f32[3,1,3,5,128]{4,2,3,1,0:T(4,128)S(1)} %copy.39), channel_id=1, source_target_pairs={{0,1},{1,2},{2,3},{3,4},{4,5},{5,6},{6,7},{7,8},{8,9},{9,10},{10,1... | collective-permute-start | bytes 69128 | tf_op jit(solution)/shard_map/ppermute | solution.py:22
where the time goes:
time: 173 us; the launch traced here: 172 us
  waiting for transfers between devices  96.1 us (56%)
  starting transfers between devices  62 us (36%)
  matrix products  6.75 us (4%)
  other arithmetic  4.55 us (3%)
  local copies, waits for them, and re-layouts  1.81 us (1%)
    ppermute x6, waiting for transfers between devices, padded_2(): lax.ppermute(head, axis, [((i + 1) % count, i) for i in range(count)])  65.1 us
    ppermute x6, starting transfers between devices, padded_2(): lax.ppermute(head, axis, [((i + 1) % count, i) for i in range(count)])  50.5 us
    ppermute x6, waiting for transfers between devices, padded_2(): lax.ppermute(tail, axis, [(i, (i + 1) % count) for i in range(count)])  31 us
    ppermute x6, starting transfers between devices, padded_2(): lax.ppermute(tail, axis, [(i, (i + 1) % count) for i in range(count)])  11.5 us
    dot_general x12, matrix products, matmul(): return jnp.matmul(left, right, precision=highest)  6.64 us
  transfers between devices with their start and end apart: 12, of which 8 were waited for; matrix products, arithmetic and copies ran while one was open for 4% of the time, Pallas kernels for 0%

commit v1 on v0

v1 whole, which is shorter than its diff:
```python
import jax
import jax.numpy as jnp
from jax import lax
from jax.experimental import pallas as pl
from jax.experimental.pallas import tpu as pltpu
from jax.sharding import PartitionSpec as P

B = 128
ATOMS = 64
time_step = 0.25
MESH = pl.DeviceIdType.MESH
f32, bf16 = jnp.float32, jnp.bfloat16

H, S, R, I = 0, 1, 2, 3
opposite = (0, 2, 1, 4, 3)


def split(x):
    high = x.astype(bf16)
    return high, (x - high.astype(f32)).astype(bf16)


def dot(a, b):
    return jnp.dot(a, b, preferred_element_type=f32)


def multiply(ah, al, bh, bl):
    return dot(ah, bh) + (dot(ah, bl) + dot(al, bh))


def neighbour(offset):
    axis = "gx" if offset <= 2 else "gy"
    count = lax.axis_size(axis)
    step = 1 if offset in (1, 3) else count - 1
    return {axis: lax.rem(lax.axis_index(axis) + step, count)}


def kernel(
    ham, inv, den, cut_hbm, der, atom_hbm,
    out, forces,
    cut, atom, own, slope, send, recv, col_send, col_recv,
    left_h, left_l, hb_h, hb_l, pair_h, pair_l, first, mixed_h, mixed_l, comm,
    in_sem, small_sem, der_sem, send_sem, recv_sem, cs_sem, cr_sem,
):
    barrier = pltpu.get_barrier_semaphore()
    places = {o: neighbour(o) for o in (1, 2, 3, 4)}
    for o in (1, 2, 3, 4):
        pl.semaphore_signal(barrier, inc=1, device_id=places[o], device_id_type=MESH)

    load_cut = pltpu.make_async_copy(cut_hbm, cut, small_sem.at[0])
    load_cut.start()
    load_atom = pltpu.make_async_copy(atom_hbm, atom, small_sem.at[1])
    load_atom.start()
    sources = {H: ham.at[0, 0], S: inv.at[0, 0], R: den.at[0, 0, 0], I: den.at[1, 0, 0]}
    loads = {}
    for m in (H, S, I, R):
        loads[m] = pltpu.make_async_copy(sources[m], own.at[m], in_sem.at[m])
        loads[m].start()
    load_slope = pltpu.make_async_copy(der.at[:, 0, 0], slope, der_sem)
    load_slope.start()

    load_cut.wait()
    keep = [None] + [cut[0, 0, o].astype(f32) for o in (1, 2, 3, 4)]

    def prepare(m):
        loads[m].wait()
        for o in range(5):
            block = own[m, o]
            if o > 0:
                block = block * keep[o]
                send[m, o - 1, 1] = block
                own[m, o] = block
            else:
                for p in range(4):
                    send[m, p, 0] = block
            high, low = split(block)
            columns = pl.ds(o * B, B)
            if m == H:
                hb_h[:, columns] = high
                hb_l[:, columns] = low
            else:
                rows = pl.ds((m - 1) * B, B)
                left_h[o, rows, :] = high
                left_l[o, rows, :] = low
                if m == S:
                    for t in range(2):
                        pair_h[t, pl.ds(B, B), columns] = high
                        pair_l[t, pl.ds(B, B), columns] = low
                else:
                    pair_h[m - 2, pl.ds(0, B), columns] = high
                    pair_l[m - 2, pl.ds(0, B), columns] = low

    copies = {}

    def transfer(m, o):
        copies[m, o] = pltpu.make_async_remote_copy(
            src_ref=send.at[m, o - 1],
            dst_ref=recv.at[m, opposite[o] - 1],
            send_sem=send_sem.at[m, o - 1],
            recv_sem=recv_sem.at[m, opposite[o] - 1],
            device_id=places[o],
            device_id_type=MESH,
        )
        copies[m, o].start()

    def arrived(m, o):
        copies[m, opposite[o]].wait_recv()

    order = (1, 2, 3, 4)
    prepare(H)
    pl.semaphore_wait(barrier, 4)
    for o in order:
        transfer(H, o)
    prepare(S)
    for o in order:
        transfer(S, o)
    prepare(I)
    for o in order:
        transfer(I, o)
    prepare(R)
    for o in order:
        transfer(R, o)

    for o in range(5):
        columns = pl.ds(o * B, B)
        first[o] = multiply(left_h[0], left_l[0], hb_h[:, columns], hb_l[:, columns])

    for o in order:
        arrived(H, o)
        near = jnp.concatenate([recv[H, o - 1, 0], recv[H, o - 1, 1]], axis=1)
        bh, bl = split(near)
        part = multiply(left_h[o], left_l[o], bh, bl)
        first[0] += part[:, B:]
        row = (first[o] + part[:, :B]) * keep[o]
        for t, sign in ((0, 1.0), (1, -1.0), (2, -1.0)):
            high, low = split(row[t * B : (t + 1) * B] * sign)
            mixed_h[o, :, pl.ds(t * B, B)] = high
            mixed_l[o, :, pl.ds(t * B, B)] = low
    for t, sign in ((0, 1.0), (1, -1.0), (2, -1.0)):
        high, low = split(first[0, pl.ds(t * B, B), :] * sign)
        mixed_h[0, :, pl.ds(t * B, B)] = high
        mixed_l[0, :, pl.ds(t * B, B)] = low

    def lefts(o, m):
        t = m - 1
        return (
            jnp.concatenate([mixed_h[o, :, pl.ds(0, B)], mixed_h[o, :, pl.ds(t * B, B)]], axis=1),
            jnp.concatenate([mixed_l[o, :, pl.ds(0, B)], mixed_l[o, :, pl.ds(t * B, B)]], axis=1),
        )

    def commutator(m):
        ah, al = lefts(0, m)
        for o in range(5):
            columns = pl.ds(o * B, B)
            comm[o] = multiply(ah, al, pair_h[m - 2, :, columns], pair_l[m - 2, :, columns])
        for o in order:
            if m == I:
                arrived(S, o)
            arrived(m, o)
            near = jnp.concatenate(
                [
                    jnp.concatenate([recv[m, o - 1, 0], recv[m, o - 1, 1]], axis=1),
                    jnp.concatenate([recv[S, o - 1, 0], recv[S, o - 1, 1]], axis=1),
                ],
                axis=0,
            )
            bh, bl = split(near)
            ah, al = lefts(o, m)
            part = multiply(ah, al, bh, bl)
            comm[0] += part[:, B:]
            comm[o] = (comm[o] + part[:, :B]) * keep[o]

    commutator(I)
    for o in range(5):
        out[0, 0, 0, o] = own[R, o] + time_step * comm[o]

    load_slope.wait()
    sends = []
    for o in order:
        block = out[0, 0, 0, o]
        for c in range(3):
            col_send[o - 1, pl.ds(c, 1), :] = jnp.sum(block * slope[c, o], axis=0, keepdims=True)
        sends.append(
            pltpu.make_async_remote_copy(
                src_ref=col_send.at[o - 1],
                dst_ref=col_recv.at[o - 1],
                send_sem=cs_sem.at[o - 1],
                recv_sem=cr_sem.at[o - 1],
                device_id=places[o],
                device_id_type=MESH,
            )
        )
        sends[-1].start()

    commutator(R)
    for o in range(5):
        out[1, 0, 0, o] = own[I, o] - time_step * comm[o]

    rows, cols = [], []
    for c in range(3):
        weighted = out[0, 0, 0, 0] * slope[c, 0]
        cols.append(jnp.sum(weighted, axis=0, keepdims=True))
        for o in order:
            weighted = weighted + out[0, 0, 0, o] * slope[c, o]
        rows.append(jnp.sum(weighted.T, axis=0, keepdims=True))
    orbital = jnp.concatenate(rows, axis=0) + jnp.concatenate(cols, axis=0)
    load_atom.wait()
    members = (
        jnp.broadcast_to(atom[0], (ATOMS, B)) == lax.broadcasted_iota(jnp.int32, (ATOMS, B), 0)
    ).astype(f32)
    for copy in sends:
        copy.wait_recv()
    for o in order:
        orbital = orbital + col_recv[o - 1, pl.ds(0, 3), :]
    total = -lax.dot_general(
        orbital, members, (((1,), (1,)), ((), ())),
        precision=lax.Precision.HIGHEST, preferred_element_type=f32,
    )
    for c in range(3):
        forces[0, c] = total[c : c + 1]
    for copy in copies.values():
        copy.wait_send()
    for copy in sends:
        copy.wait_send()


def local(hamiltonian, inverse_margin, density, cutoff, derivative, atom_of):
    hbm = pl.BlockSpec(memory_space=pltpu.HBM)
    vmem = pl.BlockSpec(memory_space=pltpu.VMEM)
    dma = pltpu.SemaphoreType.DMA
    density, forces = pl.pallas_call(
        kernel,
        out_shape=(
            jax.ShapeDtypeStruct((2, 1, 1, 5, B, B), f32),
            jax.ShapeDtypeStruct((1, 3, 1, ATOMS), f32),
        ),
        in_specs=[hbm] * 6,
        out_specs=(vmem, vmem),
        scratch_shapes=[
            pltpu.SMEM((1, 1, 5), jnp.int32),
            pltpu.VMEM((1, 1, B), jnp.int32),
            pltpu.VMEM((4, 5, B, B), f32),
            pltpu.VMEM((3, 5, B, B), f32),
            pltpu.VMEM((4, 4, 2, B, B), f32),
            pltpu.VMEM((4, 4, 2, B, B), f32),
            pltpu.VMEM((4, 8, B), f32),
            pltpu.VMEM((4, 8, B), f32),
            pltpu.VMEM((5, 3 * B, B), bf16),
            pltpu.VMEM((5, 3 * B, B), bf16),
            pltpu.VMEM((B, 5 * B), bf16),
            pltpu.VMEM((B, 5 * B), bf16),
            pltpu.VMEM((2, 2 * B, 5 * B), bf16),
            pltpu.VMEM((2, 2 * B, 5 * B), bf16),
            pltpu.VMEM((5, 3 * B, B), f32),
            pltpu.VMEM((5, B, 3 * B), bf16),
            pltpu.VMEM((5, B, 3 * B), bf16),
            pltpu.VMEM((5, B, B), f32),
            dma((4,)),
            dma((2,)),
            dma,
            dma((4, 4)),
            dma((4, 4)),
            dma((4,)),
            dma((4,)),
        ],
        compiler_params=pltpu.CompilerParams(
            collective_id=0, has_side_effects=True, vmem_limit_bytes=40 * 1024 * 1024
        ),
        name="cell",
    )(*[
        pltpu.with_memory_space_constraint(x, pltpu.HBM)
        for x in (hamiltonian, inverse_margin, density, cutoff, derivative, atom_of)
    ])
    return density, forces.reshape(1, 1, 3, ATOMS)


def solution(mesh):
    placed = (
        P("gx", "gy", None, None, None),
        P("gx", "gy", None, None, None),
        P(None, "gx", "gy", None, None, None),
        P("gx", "gy", None),
        P(None, "gx", "gy", None, None, None),
        P("gx", "gy", None),
    )
    return jax.shard_map(
        local,
        mesh=mesh,
        in_specs=placed,
        out_specs=(P(None, "gx", "gy", None, None, None), P("gx", "gy", None, None)),
        check_vma=False,
    )
```

time: 173 us -> 51 us (0.29)
  waiting for transfers between devices: 96.1 us -> 0 us
  starting transfers between devices: 62 us -> 0 us
  Pallas kernels: 0 us -> 48.8 us
  matrix products: 6.75 us -> 0 us
  other arithmetic: 4.55 us -> 0 us
    ppermute x12 -> x0, waiting for transfers between devices: 96.1 us -> none  [the longest x6 65.1 us: padded_2(): lax.ppermute(head, axis, [((i + 1) % count, i) for i in range(count)])]
    ppermute x12 -> x0, starting transfers between devices: 62 us -> none  [the longest x6 50.5 us: padded_2(): lax.ppermute(head, axis, [((i + 1) % count, i) for i in range(count)])]
    pallas_call x0 -> x1, Pallas kernels: none -> 48.8 us  [local(): pl.pallas_call(kernel, out_shape=(jax.ShapeDtypeStruct((2, 1, 1, 5, B, B)...]
    dot_general x13 -> x0, matrix products: 6.75 us -> none  [the longest x12 6.64 us: matmul(): return jnp.matmul(left, right, precision=highest)]
    mul x6 -> x0, other arithmetic: 1.74 us -> none  [the longest x1 1.19 us: local(): ham = hamiltonian[0, 0] * weight]
  transfers between devices with their start and end apart: 12 -> 0, of which waited for: 8 -> 0; matrix products, arithmetic and copies ran while one was open for 4% -> 0% of each run, Pallas kernels for 0% -> 0%
where the time goes in v1:
time: 51 us; the launch traced here: 50.9 us
  Pallas kernels  48.8 us (96%)
  local copies, waits for them, and re-layouts  1.4 us (3%)
  between operations  0.64 us (1%)
    pallas_call x1, Pallas kernels, local(): pl.pallas_call(kernel, out_shape=(jax.ShapeDtypeStruct((2, 1, 1, 5, B, B)...  48.8 us
    unnamed x2, local copies, waits for them, and re-layouts  1.4 us

profile of v1, /device:TPU:8, one launch (start us, length us, event | category | flops | bytes accessed | tf_op | source)
XLA Modules:
  0.0 50.9 jit_solution(3412590414155174160)
XLA Ops:
  0.6 48.8 %cell.1 = (f32[2,1,1,5,128,128]{5,4,3,2,1,0:T(8,128)S(1)}, f32[1,3,1,64]{3,2,1,0:T(1,128)S(1)}) custom-call(f32[1,1,5,128,128]{4,3,2,1,0:T(8,128)} %ham.1, f32[1,1,5,128,128]{4,3,2,1,0:T(8,128)} %inv.1, f32[2,1,1,5,128,128]{5,4,3,2,1,0:T(8,128)} %den.1, s32[1,1,5]{2,1,0:T(1,128)} %cut_hbm.1, f32[3,1,1,5,128,128]{5,4,3,2,1,0:T(8,128)} %der.1, ...), custom_call_target="tpu_custom_call" | custom-call | tf_op jit(solution)/shard_map/cell/pallas_call | solution.py:231
  49.5 0.8 %copy.11 = f32[2,1,1,5,128,128]{5,4,3,2,1,0:T(8,128)} copy(f32[2,1,1,5,128,128]{5,4,3,2,1,0:T(8,128)S(1)} %get-tuple-element.10) | data formatting | bytes 1310720
  50.3 0.6 %copy.12 = f32[1,1,3,64]{3,1,2,0:T(1,128)} copy(f32[1,1,3,64]{3,1,2,0:T(1,128)S(1)} %bitcast.3) | data formatting | bytes 1536

commit v2 on v1

--- a/solution.py
+++ b/solution.py
@@ -12,6 +12,7 @@
 f32, bf16 = jnp.float32, jnp.bfloat16
 
 H, S, R, I = 0, 1, 2, 3
+STAGED = (H, S)
 opposite = (0, 2, 1, 4, 3)
 
 
@@ -39,13 +40,38 @@
     ham, inv, den, cut_hbm, der, atom_hbm,
     out, forces,
     cut, atom, own, slope, send, recv, col_send, col_recv,
-    left_h, left_l, hb_h, hb_l, pair_h, pair_l, first, mixed_h, mixed_l, comm,
-    in_sem, small_sem, der_sem, send_sem, recv_sem, cs_sem, cr_sem,
+    left_h, left_l, hb_h, hb_l, pair_h, pair_l, hams, mixed_h, mixed_l, comm,
+    in_sem, small_sem, der_sem, send_sem, recv_sem, cs_sem, cr_sem, passing, pass_sem, forward_sem,
 ):
     barrier = pltpu.get_barrier_semaphore()
     places = {o: neighbour(o) for o in (1, 2, 3, 4)}
+
+    count = lax.axis_size("gx")
+    half = count // 2
+    row, line = lax.axis_index("gx"), lax.axis_index("gy")
+
+    def is_early(place):
+        at_row, at_line = place.get("gx", row), place.get("gy", line)
+        return (lax.rem(at_row, half) == 0) & ((at_row > 0) | (at_line > 0))
+
+    early = is_early({})
+    late = jnp.logical_not(early)
+    near_early = {o: is_early(places[o]) for o in (1, 2, 3, 4)}
+    near_late = {o: jnp.logical_not(near_early[o]) for o in (1, 2, 3, 4)}
+    paired = (lax.rem(row, half) == 0) & (line > 0)
+    served = (lax.rem(row, half) == half - 1) & (line > 0)
+    twin = {"gx": lax.rem(row + half, count)}
+    behind = {"gx": lax.rem(row + half - 1, count)}
+    ahead = {"gx": lax.rem(row + half + 1, count)}
+
+    def greet(place, condition):
+        @pl.when(condition)
+        def _():
+            pl.semaphore_signal(barrier, inc=1, device_id=place, device_id_type=MESH)
+
     for o in (1, 2, 3, 4):
-        pl.semaphore_signal(barrier, inc=1, device_id=places[o], device_id_type=MESH)
+        greet(places[o], early == near_early[o])
+    greet(twin, paired)
 
     load_cut = pltpu.make_async_copy(cut_hbm, cut, small_sem.at[0])
     load_cut.start()
@@ -90,10 +116,8 @@
                     pair_h[m - 2, pl.ds(0, B), columns] = high
                     pair_l[m - 2, pl.ds(0, B), columns] = low
 
-    copies = {}
-
-    def transfer(m, o):
-        copies[m, o] = pltpu.make_async_remote_copy(
+    def copy(m, o):
+        return pltpu.make_async_remote_copy(
             src_ref=send.at[m, o - 1],
             dst_ref=recv.at[m, opposite[o] - 1],
             send_sem=send_sem.at[m, o - 1],
@@ -101,43 +125,105 @@
             device_id=places[o],
             device_id_type=MESH,
         )
-        copies[m, o].start()
 
     def arrived(m, o):
-        copies[m, opposite[o]].wait_recv()
-
-    order = (1, 2, 3, 4)
+        copy(m, opposite[o]).wait_recv()
+
+    order = (3, 4, 1, 2)
+
+    as_one = paired.astype(jnp.int32)
+    heard = near_early[3].astype(jnp.int32) + near_early[4].astype(jnp.int32) + as_one
+
+    @pl.when(early)
+    def _():
+        pl.semaphore_wait(barrier, heard)
+
+    for o in (1, 2, 3, 4):
+        greet(places[o], early & near_late[o])
+    greet(behind, paired)
+
     prepare(H)
-    pl.semaphore_wait(barrier, 4)
-    for o in order:
-        transfer(H, o)
-    prepare(S)
-    for o in order:
-        transfer(S, o)
-    prepare(I)
-    for o in order:
-        transfer(I, o)
-    prepare(R)
-    for o in order:
-        transfer(R, o)
+
+    @pl.when(late)
+    def _():
+        pl.semaphore_wait(barrier, 4 + served.astype(jnp.int32))
+
+    for o in (1, 2, 3, 4):
+        greet(places[o], late & near_early[o])
+    greet(ahead, served)
+
+    def to_twin(m):
+        return pltpu.make_async_remote_copy(
+            src_ref=send.at[m, 1],
+            dst_ref=passing.at[m],
+            send_sem=send_sem.at[m, 1],
+            recv_sem=pass_sem.at[m],
+            device_id=twin,
+            device_id_type=MESH,
+        )
+
+    def forward(m):
+        return pltpu.make_async_remote_copy(
+            src_ref=passing.at[m],
+            dst_ref=recv.at[m, 0],
+            send_sem=forward_sem.at[m],
+            recv_sem=recv_sem.at[m, 0],
+            device_id=behind,
+            device_id_type=MESH,
+        )
+
+    def transfer(m, o, condition):
+        if o == 2 and m in STAGED:
+            condition = condition & jnp.logical_not(paired)
+
+        @pl.when(condition)
+        def _():
+            copy(m, o).start()
+
+    def launch(m):
+        for o in (1, 2, 3, 4):
+            transfer(m, o, late | near_early[o])
+        if m in STAGED:
+
+            @pl.when(paired)
+            def _():
+                to_twin(m).start()
+
+    launch(H)
+    for m in (S, I, R):
+        prepare(m)
+        launch(m)
+
+    @pl.when(early)
+    def _():
+        pl.semaphore_wait(barrier, 4 + 2 * as_one - heard)
+        for m in (H, S, I, R):
+            for o in (1, 2, 3, 4):
+                transfer(m, o, near_late[o])
+            if m in STAGED:
+
+                @pl.when(paired)
+                def _():
+                    to_twin(m).wait_recv()
+                    forward(m).start()
 
     for o in range(5):
         columns = pl.ds(o * B, B)
-        first[o] = multiply(left_h[0], left_l[0], hb_h[:, columns], hb_l[:, columns])
+        hams[o] = multiply(left_h[0], left_l[0], hb_h[:, columns], hb_l[:, columns])
 
     for o in order:
         arrived(H, o)
         near = jnp.concatenate([recv[H, o - 1, 0], recv[H, o - 1, 1]], axis=1)
         bh, bl = split(near)
         part = multiply(left_h[o], left_l[o], bh, bl)
-        first[0] += part[:, B:]
-        row = (first[o] + part[:, :B]) * keep[o]
+        hams[0] += part[:, B:]
+        block = (hams[o] + part[:, :B]) * keep[o]
         for t, sign in ((0, 1.0), (1, -1.0), (2, -1.0)):
-            high, low = split(row[t * B : (t + 1) * B] * sign)
+            high, low = split(block[t * B : (t + 1) * B] * sign)
             mixed_h[o, :, pl.ds(t * B, B)] = high
             mixed_l[o, :, pl.ds(t * B, B)] = low
     for t, sign in ((0, 1.0), (1, -1.0), (2, -1.0)):
-        high, low = split(first[0, pl.ds(t * B, B), :] * sign)
+        high, low = split(hams[0, pl.ds(t * B, B), :] * sign)
         mixed_h[0, :, pl.ds(t * B, B)] = high
         mixed_l[0, :, pl.ds(t * B, B)] = low
 
@@ -208,8 +294,8 @@
     members = (
         jnp.broadcast_to(atom[0], (ATOMS, B)) == lax.broadcasted_iota(jnp.int32, (ATOMS, B), 0)
     ).astype(f32)
-    for copy in sends:
-        copy.wait_recv()
+    for item in sends:
+        item.wait_recv()
     for o in order:
         orbital = orbital + col_recv[o - 1, pl.ds(0, 3), :]
     total = -lax.dot_general(
@@ -218,10 +304,16 @@
     )
     for c in range(3):
         forces[0, c] = total[c : c + 1]
-    for copy in copies.values():
-        copy.wait_send()
-    for copy in sends:
-        copy.wait_send()
+    for m in (H, S, I, R):
+        for o in order:
+            copy(m, o).wait_send()
+    for item in sends:
+        item.wait_send()
+
+    @pl.when(paired)
+    def _():
+        for m in STAGED:
+            forward(m).wait_send()
 
 
 def local(hamiltonian, inverse_margin, density, cutoff, derivative, atom_of):
@@ -262,6 +354,9 @@
             dma((4, 4)),
             dma((4,)),
             dma((4,)),
+            pltpu.VMEM((4, 2, B, B), f32),
+            dma((4,)),
+            dma((4,)),
         ],
         compiler_params=pltpu.CompilerParams(
             collective_id=0, has_side_effects=True, vmem_limit_bytes=40 * 1024 * 1024

time: 51 us -> 46.5 us (0.912)
  the two profiles are of different devices: /device:TPU:8 before, /device:TPU:55 now
where the time goes in v2:
time: 46.5 us; the launch traced here: 46.3 us
  Pallas kernels  44.3 us (95%)
  local copies, waits for them, and re-layouts  1.4 us (3%)
  between operations  0.64 us (1%)
    pallas_call x1, Pallas kernels, local(): pl.pallas_call(kernel, out_shape=(jax.ShapeDtypeStruct((2, 1, 1, 5, B, B)...  44.3 us
    unnamed x2, local copies, waits for them, and re-layouts  1.4 us

profile of v2, /device:TPU:55, one launch (start us, length us, event | category | flops | bytes accessed | tf_op | source)
XLA Modules:
  0.0 46.3 jit_solution(2492465824394359147)
XLA Ops:
  0.6 44.3 %cell.1 = (f32[2,1,1,5,128,128]{5,4,3,2,1,0:T(8,128)S(1)}, f32[1,3,1,64]{3,2,1,0:T(1,128)S(1)}) custom-call(f32[1,1,5,128,128]{4,3,2,1,0:T(8,128)} %ham.1, f32[1,1,5,128,128]{4,3,2,1,0:T(8,128)} %inv.1, f32[2,1,1,5,128,128]{5,4,3,2,1,0:T(8,128)} %den.1, s32[1,1,5]{2,1,0:T(1,128)} %cut_hbm.1, f32[3,1,1,5,128,128]{5,4,3,2,1,0:T(8,128)} %der.1, ...), custom_call_target="tpu_custom_call" | custom-call | tf_op jit(solution)/shard_map/cell/pallas_call | solution.py:323
  44.9 0.8 %copy.11 = f32[2,1,1,5,128,128]{5,4,3,2,1,0:T(8,128)} copy(f32[2,1,1,5,128,128]{5,4,3,2,1,0:T(8,128)S(1)} %get-tuple-element.10) | data formatting | bytes 1310720
  45.8 0.6 %copy.12 = f32[1,1,3,64]{3,1,2,0:T(1,128)} copy(f32[1,1,3,64]{3,1,2,0:T(1,128)S(1)} %bitcast.3) | data formatting | bytes 1536

commit v3 on v2

--- a/solution.py
+++ b/solution.py
@@ -12,7 +12,7 @@
 f32, bf16 = jnp.float32, jnp.bfloat16
 
 H, S, R, I = 0, 1, 2, 3
-STAGED = (H, S)
+BY_TWIN = (H, S)
 opposite = (0, 2, 1, 4, 3)
 
 
@@ -50,27 +50,45 @@
     half = count // 2
     row, line = lax.axis_index("gx"), lax.axis_index("gy")
 
-    def is_early(place):
-        at_row, at_line = place.get("gx", row), place.get("gy", line)
-        return (lax.rem(at_row, half) == 0) & ((at_row > 0) | (at_line > 0))
-
-    early = is_early({})
-    late = jnp.logical_not(early)
-    near_early = {o: is_early(places[o]) for o in (1, 2, 3, 4)}
-    near_late = {o: jnp.logical_not(near_early[o]) for o in (1, 2, 3, 4)}
-    paired = (lax.rem(row, half) == 0) & (line > 0)
-    served = (lax.rem(row, half) == half - 1) & (line > 0)
-    twin = {"gx": lax.rem(row + half, count)}
-    behind = {"gx": lax.rem(row + half - 1, count)}
-    ahead = {"gx": lax.rem(row + half + 1, count)}
+    def is_front(place):
+        return lax.rem(place.get("gx", row), half) == 0
+
+    def is_lead(place):
+        return (place.get("gx", row) == 0) & (place.get("gy", line) == 0)
+
+    def along(step):
+        return {"gx": lax.rem(row + step, count)}
+
+    front, lead = is_front({}), is_lead({})
+    early, late = front & jnp.logical_not(lead), jnp.logical_not(front)
+    near_front = {o: is_front(places[o]) for o in (1, 2, 3, 4)}
+    near_lead = {o: is_lead(places[o]) for o in (1, 2, 3, 4)}
+    beside = early & (near_lead[3] | near_lead[4])
+    depth = lax.rem(row, half)
+    paired = front & (line > 0)
+    carrier = (depth == 1) & (line > 0)
+    served = (depth == half - 1) & (line > 0)
+    twin, cousin, behind = along(half), along(half + 1), along(half - 1)
+    giver, taker = along(half - 1), along(half - 2)
+    ahead, helper = along(half + 1), along(half + 2)
+
+    def number(condition):
+        return condition.astype(jnp.int32)
 
     def greet(place, condition):
         @pl.when(condition)
         def _():
             pl.semaphore_signal(barrier, inc=1, device_id=place, device_id_type=MESH)
 
-    for o in (1, 2, 3, 4):
-        greet(places[o], early == near_early[o])
+    def await_greetings(condition, amount):
+        @pl.when(condition)
+        def _():
+            pl.semaphore_wait(barrier, amount)
+
+    for o in (1, 2):
+        greet(places[o], late & jnp.logical_not(near_front[o]))
+    for o in (3, 4):
+        greet(places[o], late | (early & jnp.logical_not(near_lead[o])))
     greet(twin, paired)
 
     load_cut = pltpu.make_async_copy(cut_hbm, cut, small_sem.at[0])
@@ -131,34 +149,28 @@
 
     order = (3, 4, 1, 2)
 
-    as_one = paired.astype(jnp.int32)
-    heard = near_early[3].astype(jnp.int32) + near_early[4].astype(jnp.int32) + as_one
-
-    @pl.when(early)
-    def _():
-        pl.semaphore_wait(barrier, heard)
-
-    for o in (1, 2, 3, 4):
-        greet(places[o], early & near_late[o])
-    greet(behind, paired)
-
+    await_greetings(early, 2 - number(beside) + number(paired))
+    await_greetings(lead, 2)
+    for o in (3, 4):
+        greet(places[o], lead)
+    greet(places[1], front)
+    greet(cousin, paired)
     prepare(H)
-
-    @pl.when(late)
-    def _():
-        pl.semaphore_wait(barrier, 4 + served.astype(jnp.int32))
-
-    for o in (1, 2, 3, 4):
-        greet(places[o], late & near_early[o])
+    await_greetings(late, 4 + number(carrier) + 2 * number(served))
+    for o in (1, 2):
+        greet(places[o], late & near_front[o])
+    greet(giver, carrier)
+    greet(taker, carrier)
     greet(ahead, served)
-
-    def to_twin(m):
+    greet(helper, served)
+
+    def hand_on(m):
         return pltpu.make_async_remote_copy(
             src_ref=send.at[m, 1],
             dst_ref=passing.at[m],
             send_sem=send_sem.at[m, 1],
             recv_sem=pass_sem.at[m],
-            device_id=twin,
+            device_id=twin if m in BY_TWIN else cousin,
             device_id_type=MESH,
         )
 
@@ -168,44 +180,63 @@
             dst_ref=recv.at[m, 0],
             send_sem=forward_sem.at[m],
             recv_sem=recv_sem.at[m, 0],
-            device_id=behind,
+            device_id=behind if m in BY_TWIN else taker,
             device_id_type=MESH,
         )
 
     def transfer(m, o, condition):
-        if o == 2 and m in STAGED:
-            condition = condition & jnp.logical_not(paired)
-
         @pl.when(condition)
         def _():
             copy(m, o).start()
 
-    def launch(m):
-        for o in (1, 2, 3, 4):
-            transfer(m, o, late | near_early[o])
-        if m in STAGED:
+    def pass_on(m):
+        hand_on(m).wait_recv()
+        forward(m).start()
+
+    def launch(m, which):
+        for o in (1, 2):
+            transfer(m, o, late & which)
+        for o in (3, 4):
+            transfer(m, o, jnp.logical_not(early & near_lead[o]) & which)
+        if m in BY_TWIN:
 
             @pl.when(paired)
             def _():
-                to_twin(m).start()
-
-    launch(H)
-    for m in (S, I, R):
+                hand_on(m).start()
+
+    launch(H, True)
+    for m in (S, I):
         prepare(m)
-        launch(m)
-
-    @pl.when(early)
-    def _():
-        pl.semaphore_wait(barrier, 4 + 2 * as_one - heard)
+        launch(m, True)
+    prepare(R)
+    launch(R, front)
+
+    await_greetings(front, 1 + number(paired))
+    for m in (H, S, I, R):
+        transfer(m, 1, front)
+        if m not in BY_TWIN:
+
+            @pl.when(paired)
+            def _():
+                hand_on(m).start()
+
+    for o in (3, 4):
+        greet(places[o], early & near_lead[o])
+    await_greetings(beside, 1)
+    for o in (3, 4):
         for m in (H, S, I, R):
-            for o in (1, 2, 3, 4):
-                transfer(m, o, near_late[o])
-            if m in STAGED:
-
-                @pl.when(paired)
-                def _():
-                    to_twin(m).wait_recv()
-                    forward(m).start()
+            transfer(m, o, early & near_lead[o])
+
+    greet(places[2], front)
+    greet(behind, paired)
+    await_greetings(front, 1 + number(paired))
+    for m in (H, S, I):
+        transfer(m, 2, front & jnp.logical_not(paired))
+    for m in BY_TWIN:
+
+        @pl.when(paired)
+        def _():
+            pass_on(m)
 
     for o in range(5):
         columns = pl.ds(o * B, B)
@@ -239,6 +270,13 @@
         for o in range(5):
             columns = pl.ds(o * B, B)
             comm[o] = multiply(ah, al, pair_h[m - 2, :, columns], pair_l[m - 2, :, columns])
+        if m == I:
+            @pl.when(late)
+            def _():
+                for o in (1, 2, 3, 4):
+                    copy(I, o).wait_send()
+                    copy(R, o).start()
+
         for o in order:
             if m == I:
                 arrived(S, o)
@@ -257,6 +295,7 @@
             comm[o] = (comm[o] + part[:, :B]) * keep[o]
 
     commutator(I)
+    transfer(R, 2, front & jnp.logical_not(paired))
     for o in range(5):
         out[0, 0, 0, o] = own[R, o] + time_step * comm[o]
 
@@ -277,6 +316,13 @@
             )
         )
         sends[-1].start()
+
+    @pl.when(carrier)
+    def _():
+        pl.semaphore_wait(barrier, 1)
+        for m in (I, R, S, H):
+            if m not in BY_TWIN:
+                pass_on(m)
 
     commutator(R)
     for o in range(5):
@@ -304,15 +350,22 @@
     )
     for c in range(3):
         forces[0, c] = total[c : c + 1]
-    for m in (H, S, I, R):
+    for m in (H, S, R):
         for o in order:
             copy(m, o).wait_send()
+
+    @pl.when(front)
+    def _():
+        for o in order:
+            copy(I, o).wait_send()
+
     for item in sends:
         item.wait_send()
 
-    @pl.when(paired)
-    def _():
-        for m in STAGED:
+    for m in (H, S, I, R):
+
+        @pl.when(paired if m in BY_TWIN else carrier)
+        def _():
             forward(m).wait_send()
 
 

time: 46.5 us -> 43.7 us (0.940)
  Pallas kernels: 44.3 us -> 41.5 us
    pallas_call x1, Pallas kernels: 44.3 us -> 41.5 us  [local(): pl.pallas_call(kernel, out_shape=(jax.ShapeDtypeStruct((2, 1, 1, 5, B, B)...]
where the time goes in v3:
time: 43.7 us; the launch traced here: 43.6 us
  Pallas kernels  41.5 us (95%)
  local copies, waits for them, and re-layouts  1.4 us (3%)
  between operations  0.64 us (1%)
    pallas_call x1, Pallas kernels, local(): pl.pallas_call(kernel, out_shape=(jax.ShapeDtypeStruct((2, 1, 1, 5, B, B)...  41.5 us
    unnamed x2, local copies, waits for them, and re-layouts  1.4 us

profile of v3, /device:TPU:55, one launch (start us, length us, event | category | flops | bytes accessed | tf_op | source)
XLA Modules:
  0.0 43.6 jit_solution(11640338915230536401)
XLA Ops:
  0.6 41.5 %cell.1 = (f32[2,1,1,5,128,128]{5,4,3,2,1,0:T(8,128)S(1)}, f32[1,3,1,64]{3,2,1,0:T(1,128)S(1)}) custom-call(f32[1,1,5,128,128]{4,3,2,1,0:T(8,128)} %ham.1, f32[1,1,5,128,128]{4,3,2,1,0:T(8,128)} %inv.1, f32[2,1,1,5,128,128]{5,4,3,2,1,0:T(8,128)} %den.1, s32[1,1,5]{2,1,0:T(1,128)} %cut_hbm.1, f32[3,1,1,5,128,128]{5,4,3,2,1,0:T(8,128)} %der.1, ...), custom_call_target="tpu_custom_call" | custom-call | tf_op jit(solution)/shard_map/cell/pallas_call | solution.py:376
  42.2 0.8 %copy.11 = f32[2,1,1,5,128,128]{5,4,3,2,1,0:T(8,128)} copy(f32[2,1,1,5,128,128]{5,4,3,2,1,0:T(8,128)S(1)} %get-tuple-element.10) | data formatting | bytes 1310720
  43.0 0.6 %copy.12 = f32[1,1,3,64]{3,1,2,0:T(1,128)} copy(f32[1,1,3,64]{3,1,2,0:T(1,128)S(1)} %bitcast.3) | data formatting | bytes 1536

commit v4 on v3

--- a/solution.py
+++ b/solution.py
@@ -41,7 +41,7 @@
     out, forces,
     cut, atom, own, slope, send, recv, col_send, col_recv,
     left_h, left_l, hb_h, hb_l, pair_h, pair_l, hams, mixed_h, mixed_l, comm,
-    in_sem, small_sem, der_sem, send_sem, recv_sem, cs_sem, cr_sem, passing, pass_sem, forward_sem,
+    in_sem, small_sem, der_sem, send_sem, recv_sem, cs_sem, cr_sem, passing, pass_sem, forward_sem, side_h, side_l,
 ):
     barrier = pltpu.get_barrier_semaphore()
     places = {o: neighbour(o) for o in (1, 2, 3, 4)}
@@ -67,7 +67,8 @@
     depth = lax.rem(row, half)
     paired = front & (line > 0)
     carrier = (depth == 1) & (line > 0)
-    served = (depth == half - 1) & (line > 0)
+    last = depth == half - 1
+    served = last & (line > 0)
     twin, cousin, behind = along(half), along(half + 1), along(half - 1)
     giver, taker = along(half - 1), along(half - 2)
     ahead, helper = along(half + 1), along(half + 2)
@@ -193,23 +194,25 @@
         hand_on(m).wait_recv()
         forward(m).start()
 
-    def launch(m, which):
+    def launch(m):
         for o in (1, 2):
-            transfer(m, o, late & which)
+            transfer(m, o, late)
         for o in (3, 4):
-            transfer(m, o, jnp.logical_not(early & near_lead[o]) & which)
+            transfer(m, o, jnp.logical_not(early & near_lead[o]) if m == H else front & jnp.logical_not(early & near_lead[o]))
         if m in BY_TWIN:
 
             @pl.when(paired)
             def _():
                 hand_on(m).start()
 
-    launch(H, True)
+    launch(H)
     for m in (S, I):
         prepare(m)
-        launch(m, True)
+        launch(m)
     prepare(R)
-    launch(R, front)
+    transfer(R, 1, last)
+    for o in (3, 4):
+        transfer(R, o, front & jnp.logical_not(early & near_lead[o]))
 
     await_greetings(front, 1 + number(paired))
     for m in (H, S, I, R):
@@ -241,6 +244,13 @@
     for o in range(5):
         columns = pl.ds(o * B, B)
         hams[o] = multiply(left_h[0], left_l[0], hb_h[:, columns], hb_l[:, columns])
+
+    @pl.when(late)
+    def _():
+        for o in (3, 4):
+            copy(H, o).wait_send()
+            copy(S, o).start()
+            copy(I, o).start()
 
     for o in order:
         arrived(H, o)
@@ -265,58 +275,58 @@
             jnp.concatenate([mixed_l[o, :, pl.ds(0, B)], mixed_l[o, :, pl.ds(t * B, B)]], axis=1),
         )
 
+    def columns_to(o):
+        return pltpu.make_async_remote_copy(
+            src_ref=col_send.at[o - 1],
+            dst_ref=col_recv.at[o - 1],
+            send_sem=cs_sem.at[o - 1],
+            recv_sem=cr_sem.at[o - 1],
+            device_id=places[o],
+            device_id_type=MESH,
+        )
+
+    def new_real(o):
+        block = own[R, o] + time_step * comm[o]
+        out[0, 0, 0, o] = block
+        for c in range(3):
+            col_send[o - 1, pl.ds(c, 1), :] = jnp.sum(block * slope[c, o], axis=0, keepdims=True)
+        columns_to(o).start()
+        transfer(R, o, late & jnp.logical_not(last) if o == 1 else late)
+
+    def near(m, o):
+        return split(jnp.concatenate([recv[m, o - 1, 0], recv[m, o - 1, 1]], axis=1))
+
+    def mixed(o, t):
+        return mixed_h[o, :, pl.ds(t * B, B)], mixed_l[o, :, pl.ds(t * B, B)]
+
     def commutator(m):
         ah, al = lefts(0, m)
         for o in range(5):
             columns = pl.ds(o * B, B)
             comm[o] = multiply(ah, al, pair_h[m - 2, :, columns], pair_l[m - 2, :, columns])
-        if m == I:
-            @pl.when(late)
-            def _():
-                for o in (1, 2, 3, 4):
-                    copy(I, o).wait_send()
-                    copy(R, o).start()
-
-        for o in order:
+        for o in (1, 3, 4, 2):
             if m == I:
                 arrived(S, o)
-            arrived(m, o)
-            near = jnp.concatenate(
-                [
-                    jnp.concatenate([recv[m, o - 1, 0], recv[m, o - 1, 1]], axis=1),
-                    jnp.concatenate([recv[S, o - 1, 0], recv[S, o - 1, 1]], axis=1),
-                ],
-                axis=0,
-            )
-            bh, bl = split(near)
-            ah, al = lefts(o, m)
-            part = multiply(ah, al, bh, bl)
-            comm[0] += part[:, B:]
-            comm[o] = (comm[o] + part[:, :B]) * keep[o]
-
-    commutator(I)
-    transfer(R, 2, front & jnp.logical_not(paired))
-    for o in range(5):
-        out[0, 0, 0, o] = own[R, o] + time_step * comm[o]
+                sh, sl = near(S, o)
+                side_h[o - 1], side_l[o - 1] = sh, sl
+                arrived(I, o)
+                bh, bl = near(I, o)
+                part = multiply(*lefts(o, m), jnp.concatenate([bh, sh], axis=0), jnp.concatenate([bl, sl], axis=0))
+                comm[0] += part[:, B:]
+                comm[o] = (comm[o] + part[:, :B]) * keep[o]
+                new_real(o)
+            else:
+                part = multiply(*mixed(o, 1), side_h[o - 1], side_l[o - 1])
+                comm[0] += part[:, B:]
+                comm[o] += part[:, :B]
+        if m == R:
+            for o in (1, 3, 4, 2):
+                arrived(R, o)
+                part = multiply(*mixed(o, 0), *near(R, o))
+                comm[0] += part[:, B:]
+                out[1, 0, 0, o] = own[I, o] - time_step * ((comm[o] + part[:, :B]) * keep[o])
 
     load_slope.wait()
-    sends = []
-    for o in order:
-        block = out[0, 0, 0, o]
-        for c in range(3):
-            col_send[o - 1, pl.ds(c, 1), :] = jnp.sum(block * slope[c, o], axis=0, keepdims=True)
-        sends.append(
-            pltpu.make_async_remote_copy(
-                src_ref=col_send.at[o - 1],
-                dst_ref=col_recv.at[o - 1],
-                send_sem=cs_sem.at[o - 1],
-                recv_sem=cr_sem.at[o - 1],
-                device_id=places[o],
-                device_id_type=MESH,
-            )
-        )
-        sends[-1].start()
-
     @pl.when(carrier)
     def _():
         pl.semaphore_wait(barrier, 1)
@@ -324,9 +334,9 @@
             if m not in BY_TWIN:
                 pass_on(m)
 
-    commutator(R)
-    for o in range(5):
-        out[1, 0, 0, o] = own[I, o] - time_step * comm[o]
+    commutator(I)
+    transfer(R, 2, front & jnp.logical_not(paired))
+    out[0, 0, 0, 0] = own[R, 0] + time_step * comm[0]
 
     rows, cols = [], []
     for c in range(3):
@@ -340,8 +350,11 @@
     members = (
         jnp.broadcast_to(atom[0], (ATOMS, B)) == lax.broadcasted_iota(jnp.int32, (ATOMS, B), 0)
     ).astype(f32)
-    for item in sends:
-        item.wait_recv()
+    commutator(R)
+    out[1, 0, 0, 0] = own[I, 0] - time_step * comm[0]
+
+    for o in order:
+        columns_to(o).wait_recv()
     for o in order:
         orbital = orbital + col_recv[o - 1, pl.ds(0, 3), :]
     total = -lax.dot_general(
@@ -350,17 +363,19 @@
     )
     for c in range(3):
         forces[0, c] = total[c : c + 1]
-    for m in (H, S, R):
+    for m in (S, I, R):
         for o in order:
             copy(m, o).wait_send()
+    for o in (1, 2):
+        copy(H, o).wait_send()
 
     @pl.when(front)
     def _():
-        for o in order:
-            copy(I, o).wait_send()
-
-    for item in sends:
-        item.wait_send()
+        for o in (3, 4):
+            copy(H, o).wait_send()
+
+    for o in order:
+        columns_to(o).wait_send()
 
     for m in (H, S, I, R):
 
@@ -410,6 +425,8 @@
             pltpu.VMEM((4, 2, B, B), f32),
             dma((4,)),
             dma((4,)),
+            pltpu.VMEM((4, B, 2 * B), bf16),
+            pltpu.VMEM((4, B, 2 * B), bf16),
         ],
         compiler_params=pltpu.CompilerParams(
             collective_id=0, has_side_effects=True, vmem_limit_bytes=40 * 1024 * 1024

time: 43.7 us -> 41.5 us (0.950)
  Pallas kernels: 41.5 us -> 39.3 us
    pallas_call x1, Pallas kernels: 41.5 us -> 39.3 us  [local(): pl.pallas_call(kernel, out_shape=(jax.ShapeDtypeStruct((2, 1, 1, 5, B, B)...]
where the time goes in v4:
time: 41.5 us; the launch traced here: 41.4 us
  Pallas kernels  39.3 us (95%)
  local copies, waits for them, and re-layouts  1.4 us (3%)
  between operations  0.64 us (2%)
    pallas_call x1, Pallas kernels, local(): pl.pallas_call(kernel, out_shape=(jax.ShapeDtypeStruct((2, 1, 1, 5, B, B)...  39.3 us
    unnamed x2, local copies, waits for them, and re-layouts  1.4 us

profile of v4, /device:TPU:55, one launch (start us, length us, event | category | flops | bytes accessed | tf_op | source)
XLA Modules:
  0.0 41.4 jit_solution(719676946440248709)
XLA Ops:
  0.6 39.3 %cell.1 = (f32[2,1,1,5,128,128]{5,4,3,2,1,0:T(8,128)S(1)}, f32[1,3,1,64]{3,2,1,0:T(1,128)S(1)}) custom-call(f32[1,1,5,128,128]{4,3,2,1,0:T(8,128)} %ham.1, f32[1,1,5,128,128]{4,3,2,1,0:T(8,128)} %inv.1, f32[2,1,1,5,128,128]{5,4,3,2,1,0:T(8,128)} %den.1, s32[1,1,5]{2,1,0:T(1,128)} %cut_hbm.1, f32[3,1,1,5,128,128]{5,4,3,2,1,0:T(8,128)} %der.1, ...), custom_call_target="tpu_custom_call" | custom-call | tf_op jit(solution)/shard_map/cell/pallas_call | solution.py:391
  40.0 0.8 %copy.11 = f32[2,1,1,5,128,128]{5,4,3,2,1,0:T(8,128)} copy(f32[2,1,1,5,128,128]{5,4,3,2,1,0:T(8,128)S(1)} %get-tuple-element.10) | data formatting | bytes 1310720
  40.8 0.6 %copy.12 = f32[1,1,3,64]{3,1,2,0:T(1,128)} copy(f32[1,1,3,64]{3,1,2,0:T(1,128)S(1)} %bitcast.3) | data formatting | bytes 1536

commit v5 on v4

--- a/solution.py
+++ b/solution.py
@@ -195,8 +195,9 @@
         forward(m).start()
 
     def launch(m):
-        for o in (1, 2):
-            transfer(m, o, late)
+        if m == H:
+            for o in (1, 2):
+                transfer(m, o, late)
         for o in (3, 4):
             transfer(m, o, jnp.logical_not(early & near_lead[o]) if m == H else front & jnp.logical_not(early & near_lead[o]))
         if m in BY_TWIN:
@@ -210,7 +211,6 @@
         prepare(m)
         launch(m)
     prepare(R)
-    transfer(R, 1, last)
     for o in (3, 4):
         transfer(R, o, front & jnp.logical_not(early & near_lead[o]))
 
@@ -247,10 +247,12 @@
 
     @pl.when(late)
     def _():
-        for o in (3, 4):
+        for o in (1, 2, 3, 4):
             copy(H, o).wait_send()
             copy(S, o).start()
             copy(I, o).start()
+
+    transfer(R, 1, last)
 
     for o in order:
         arrived(H, o)
@@ -357,7 +359,7 @@
         columns_to(o).wait_recv()
     for o in order:
         orbital = orbital + col_recv[o - 1, pl.ds(0, 3), :]
-    total = -lax.dot_general(
+    total = lax.dot_general(
         orbital, members, (((1,), (1,)), ((), ())),
         precision=lax.Precision.HIGHEST, preferred_element_type=f32,
     )
@@ -366,12 +368,10 @@
     for m in (S, I, R):
         for o in order:
             copy(m, o).wait_send()
-    for o in (1, 2):
-        copy(H, o).wait_send()
 
     @pl.when(front)
     def _():
-        for o in (3, 4):
+        for o in order:
             copy(H, o).wait_send()
 
     for o in order:
@@ -436,7 +436,7 @@
         pltpu.with_memory_space_constraint(x, pltpu.HBM)
         for x in (hamiltonian, inverse_margin, density, cutoff, derivative, atom_of)
     ])
-    return density, forces.reshape(1, 1, 3, ATOMS)
+    return density, -forces.reshape(1, 1, 3, ATOMS)
 
 
 def solution(mesh):

time: 41.5 us -> 41.5 us (level)
  other arithmetic: 0 us -> 0.57 us
  local copies, waits for them, and re-layouts: 1.4 us -> 0.84 us
    unnamed x0 -> x1, other arithmetic: none -> 0.57 us
    unnamed x2 -> x1, local copies, waits for them, and re-layouts: 1.4 us -> 0.84 us
where the time goes in v5:
time: 41.5 us; the launch traced here: 41.4 us
  Pallas kernels  39.3 us (95%)
  local copies, waits for them, and re-layouts  0.84 us (2%)
  between operations  0.64 us (2%)
  other arithmetic  0.57 us (1%)
    pallas_call x1, Pallas kernels, local(): pl.pallas_call(kernel, out_shape=(jax.ShapeDtypeStruct((2, 1, 1, 5, B, B)...  39.3 us
    unnamed x1, local copies, waits for them, and re-layouts  0.84 us

profile of v5, /device:TPU:55, one launch (start us, length us, event | category | flops | bytes accessed | tf_op | source)
XLA Modules:
  0.0 41.4 jit_solution(16482143450789777224)
XLA Ops:
  0.6 39.3 %cell.1 = (f32[2,1,1,5,128,128]{5,4,3,2,1,0:T(8,128)S(1)}, f32[1,3,1,64]{3,2,1,0:T(1,128)S(1)}) custom-call(f32[1,1,5,128,128]{4,3,2,1,0:T(8,128)} %ham.1, f32[1,1,5,128,128]{4,3,2,1,0:T(8,128)} %inv.1, f32[2,1,1,5,128,128]{5,4,3,2,1,0:T(8,128)} %den.1, s32[1,1,5]{2,1,0:T(1,128)} %cut_hbm.1, f32[3,1,1,5,128,128]{5,4,3,2,1,0:T(8,128)} %der.1, ...), custom_call_target="tpu_custom_call" | custom-call | tf_op jit(solution)/shard_map/cell/pallas_call | solution.py:391
  40.0 0.6 %negate_bitcast_fusion = f32[1,1,3,64]{3,1,2,0:T(1,128)} fusion(f32[1,3,1,64]{3,2,1,0:T(1,128)S(1)} %get-tuple-element.5), kind=kLoop, calls=%fused_computation | loop fusion | flops 192 | bytes 1536
  40.5 0.8 %copy.10 = f32[2,1,1,5,128,128]{5,4,3,2,1,0:T(8,128)} copy(f32[2,1,1,5,128,128]{5,4,3,2,1,0:T(8,128)S(1)} %get-tuple-element.10) | data formatting | bytes 1310720
